TPU v7x, 128 devices: a whole 4x4x4 slice. The times are simulated.
128 devices in a mesh: chan: 8 (over x, z_hi), row: 4 (over y), col: 4 (over z_lo, core).
Axes of the slice: x: 4, y: 4, z: 4 (z_hi: 2, z_lo: 2; z = z_hi * 2 + z_lo), core: 2. Of those that a mesh axis runs over, the one named last changes fastest.
Arguments:
- voltages: bfloat16 [2, 4, 512, 64, 1031], P(None, None, ('chan', 'row', 'col')), may hold values from -6 to 6
- window: float32 [8, 64], replicated, may hold values from 0.1 to 0.6
- kept_channels: int32 [48], replicated, may hold values from 0 to 63, as said below
Outputs:
- covariance: float32 [48, 2, 2048, 2048], P('chan', None, 'row', 'col')
Inputs may be any that keep to these rules, and one draw needn't show every extreme that they name: `kept_channels`: 48 distinct channel numbers of the 64-point transform, in any order.
All inputs are finite; a program needn't handle non-finite values.
Results may differ from a plain program's by a relative error of at most 0.0019.
Values may be sent and summed in bfloat16 or wider, within the bound.
No kernel may reach another device: no remote copies, remote signals or barrier semaphores. Data moves between devices by JAX's collectives and lax.ppermute only.
A program may use at most 128 MiB of HBM per device.

v0:
```python
import math
import jax
import jax.numpy as jnp
from jax import lax
from jax.sharding import Mesh
from jax.sharding import PartitionSpec as P

COL = ("col_0", "col_1")
CHAN_ROW_COL = ("chan", "row", "col_0", "col_1")
ROW_COL = ("row", "col_0", "col_1")


def in_order(tiles, dim):
    shape = list(tiles.shape[1:])
    shape[dim] *= tiles.shape[0]
    return jnp.moveaxis(tiles, 0, dim).reshape(shape)


def gather_in_order(shard, axes, turns):
    tiles = shard[None]
    for k in turns:
        tiles = lax.all_gather(tiles, axes[k], axis=0, tiled=True)
    current = [lax.axis_size(axes[k]) for k in reversed(turns)]
    tiles = tiles.reshape(*current, *shard.shape)
    turned = sorted(range(len(turns)), key=lambda place: turns[len(turns) - 1 - place])
    return tiles.transpose(*turned, *range(len(turns), tiles.ndim)).reshape(-1, *shard.shape)


def whole_of(shard, axes, turns, dim):
    return in_order(gather_in_order(shard, axes, turns), dim)


def cut_along(shard, dim, peers):
    shape = shard.shape
    tiles = shard.reshape(*shape[:dim], peers, shape[dim] // peers, *shape[dim + 1 :])
    return jnp.moveaxis(tiles, dim, 0)


def exchange_both(shard, axis, axes, splits, concats):
    sizes = [lax.axis_size(a) for a in axes]
    tiles = cut_along(shard, splits[0], sizes[0])
    tiles = jnp.moveaxis(cut_along(tiles, splits[1] + 1, sizes[1]), 0, 1)
    inside = tiles.shape[2:]
    tiles = tiles.reshape(-1, *inside)
    tiles = lax.all_to_all(tiles, axis, split_axis=0, concat_axis=0, tiled=True)
    tiles = in_order(tiles.reshape(*sizes, *inside), concats[0] + 1)
    return in_order(tiles, concats[1])


def phase_table(kept_channels, points):
    positions = jnp.arange(points, dtype=jnp.int32)
    phases = kept_channels[:, None] * positions[None, :] % points
    angles = phases.astype(jnp.float32) * (2.0 * math.pi / points)
    factor = 1.0 / math.sqrt(points)
    cosines = jnp.cos(angles) * factor
    sines = jnp.sin(angles) * factor
    return jnp.stack([jnp.stack([cosines, -sines]), jnp.stack([sines, cosines])])


def filter_bank(samples, window, frames):
    filtered = window[0][:, None] * samples[..., 0:frames]
    for tap_index in range(1, window.shape[0]):
        filtered = (
            filtered + window[tap_index][:, None] * samples[..., tap_index : tap_index + frames]
        )
    return filtered


def products(row_full, col_full):
    real_part = jnp.einsum(
        "bpmif,bpmjf->mij", row_full, col_full, preferred_element_type=jnp.float32
    )
    imag_part = jnp.einsum(
        "bmif,bmjf->mij", row_full[:, 1], col_full[:, 0], preferred_element_type=jnp.float32
    )
    imag_part = imag_part - jnp.einsum(
        "bmif,bmjf->mij", row_full[:, 0], col_full[:, 1], preferred_element_type=jnp.float32
    )
    inverse = 1.0 / (row_full.shape[0] * row_full.shape[4])
    return jnp.stack([real_part, imag_part], axis=1) * inverse


def correlate(pieces):
    row_part, col_part = pieces
    row_full = whole_of(row_part, COL, (0, 1), 0)
    col_full = lax.all_gather(col_part, "row", axis=0, tiled=True)
    return products(row_full, col_full)


def arrange(spectra, shape):
    return (spectra.reshape(shape), jnp.swapaxes(spectra, 1, 2).reshape(shape))


def shards(voltages, window, kept_channels):
    chan_count = lax.axis_size("chan")
    row_count = lax.axis_size("row")
    col_count = lax.axis_size(COL)
    points = window.shape[1]
    frames = voltages.shape[4] - window.shape[0] + 1
    slot_inputs = voltages.shape[2]
    per_chan = kept_channels.shape[0] // chan_count
    block_frames = frames // col_count
    samples = voltages.astype(jnp.float32)
    filtered = filter_bank(samples, window, frames)
    filtered = filtered.reshape(2, row_count, slot_inputs, points, col_count, block_frames)
    table = phase_table(kept_channels, points).reshape(2, 2, chan_count, per_chan, points)
    spectra = jnp.einsum(
        "qrsnbf,qpckn->crbpksf", filtered, table, precision=lax.Precision.HIGHEST
    ).astype(jnp.bfloat16)
    sectioned_shape = (
        chan_count,
        row_count * col_count,
        2,
        per_chan,
        1,
        1,
        slot_inputs,
        block_frames,
    )
    outgoing = arrange(spectra, sectioned_shape)
    arrived = (
        exchange_both(outgoing[0], CHAN_ROW_COL, ("chan", ROW_COL), (0, 1), (4, 5)),
        exchange_both(outgoing[1], CHAN_ROW_COL, ("chan", ROW_COL), (0, 1), (4, 5)),
    )
    arrived = jax.tree.map(lambda piece: piece.reshape(1, 2, per_chan, -1, block_frames), arrived)
    return correlate(arrived)


def solution(mesh):
    finer = Mesh(
        mesh.devices.reshape(mesh.shape["chan"], mesh.shape["row"], 2, 2),
        ("chan", "row", "col_0", "col_1"),
    )
    placed = (P(None, None, CHAN_ROW_COL, None, None), P(), P())
    return jax.shard_map(
        shards, mesh=finer, in_specs=placed, out_specs=P("chan", None, "row", COL), check_vma=False
    )
```

profile of v0, /device:TPU:1, one launch (start us, length us, event | category | flops | bytes accessed | tf_op | source)
XLA Modules:
  0.0 426.3 jit_solution(12734910430916442310)
XLA Ops:
  6.5 0.0 all-gather.4.cloned.1.call-start
  6.5 0.7 mul.173
  7.3 0.1 copy.31
  7.4 1.0 slice_bitcast_fusion.19
  8.3 0.2 fusion.31
  8.5 3.5 convert_element_type.36
  12.0 16.8 %fusion.2 = f32[2,4,4,64,1024]{4,3,2,1,0:T(8,128)} fusion(f32[2,4,4,64,1031]{4,3,2,1,0:T(8,128)S(1)} %convert_element_type.36, f32[64]{0:T(128)S(1)} %get-tuple-element.14, f32[64]{0:T(128)S(1)} %get-tuple-element.15, f32[64]{0:T(128)S(1)} %get-tuple-element.9, f32[64]{0:T(128)S(1)} %get-tuple-element.10, f32[64]{0:T(128)S(1)} %get-tuple-element.11, ...), kind=kLoop, calls=%fused_computation.4 | loop fusion | flops 31457280 | bytes 75499520 | tf_op jit(solution)/shard_map/add | solution.py:64
  28.8 10.6 %reshape.151 = f32[2,4,4,64,4,256]{5,4,3,2,1,0:T(4,128)} reshape(f32[2,4,4,64,1024]{4,3,2,1,0:T(8,128)} %fusion.2) | data formatting | bytes 16777216 | tf_op jit(solution)/shard_map/reshape | solution.py:105
  39.4 9.3 %bitcast_convert_fusion = bf16[2,8,6,4,4,4,256]{6,1,5,4,3,2,0:T(8,128)(2,1)S(1)} fusion(f32[2,4,4,64,4,256,1,1]{5,4,3,2,1,0,7,6:T(4,128)} %bitcast.102, f32[1,1,8,6,64]{4,2,0,3,1:T(8,128)S(1)} %get-tuple-element.7, f32[1,1,8,6,64]{4,2,0,3,1:T(8,128)S(1)} %get-tuple-element.6, f32[1,1,8,6,64]{4,2,0,3,1:T(8,128)S(1)} %get-tuple-element.5), kind=kOutput, calls=%fused_computation.28 | convolution fusion | flops 2417528832 | bytes 11571200 | tf_op jit(solution)/shard_map/qrsnbf,qpckn->crbpksf/dot_general | solution.py:107
  48.7 2.4 copy.33
  51.1 52.5 %all_to_all.10 = bf16[128,1,1,2,6,1,1,4,256]{8,7,4,3,6,5,2,1,0:T(4,128)(2,1)S(1)} all-to-all(bf16[128,1,1,2,6,1,1,4,256]{8,7,4,3,6,5,2,1,0:T(4,128)(2,1)S(1)} %bitcast.101), channel_id=1, replica_groups=mesh['chan'=8,'row'=4,'col_0'=2,'col_1'=2] {'chan','row','col_0','col_1'}, dimensions={0} | all-to-all | bytes 6291456 | tf_op jit(solution)/shard_map/all_to_all | solution.py:45
  103.7 3.3 copy.35
  106.9 2.2 copy.36
  109.1 0.0 all-gather.4.cloned.1.call-update
  109.1 0.0 all-gather.6.cloned.1.call-start
  109.2 79.7 %all-gather.4.cloned.1.call-done = bf16[2,1,2,6,512,256]{5,4,3,2,1,0:T(8,128)(2,1)} async-done(((bf16[1,1,2,6,512,256]{5,4,3,2,1,0:T(8,128)(2,1)}), bf16[2,1,2,6,512,256]{5,4,3,2,1,0:T(8,128)(2,1)}) %all-gather.4.cloned.1.call-update) | async-done | bytes 6291472 | tf_op jit(solution)/shard_map/all_gather | solution.py:22
  188.9 0.0 all-gather.6.cloned.1.call-update
  188.9 0.0 all-gather.8.cloned.1.call-start
  188.9 2.4 copy.38
  191.4 50.3 %all_to_all.11 = bf16[128,1,1,2,6,1,1,4,256]{8,7,4,3,6,5,2,1,0:T(4,128)(2,1)S(1)} all-to-all(bf16[128,1,1,2,6,1,1,4,256]{8,7,4,3,6,5,2,1,0:T(4,128)(2,1)S(1)} %bitcast.99), channel_id=1, replica_groups=mesh['chan'=8,'row'=4,'col_0'=2,'col_1'=2] {'chan','row','col_0','col_1'}, dimensions={0} | all-to-all | bytes 6291456 | tf_op jit(solution)/shard_map/all_to_all | solution.py:45
  241.6 1.7 copy.40
  243.4 3.0 reshape_reshape.7
  246.4 0.0 all-gather.8.cloned.1.call-update
  246.4 0.0 all-gather.6.cloned.1.call-done
  246.5 10.8 %copy.37 = bf16[2,2,1,2,6,512,256]{6,5,3,4,1,0,2:T(8,128)(2,1)} copy(bf16[2,2,1,2,6,512,256]{6,5,4,3,0,1,2:T(8,128)(2,1)} %bitcast.91) | data formatting | bytes 25165824 | tf_op jit(solution)/shard_map/transpose | solution.py:26
  257.3 104.5 %all-gather.8.cloned.1.call-done = bf16[4,2,6,512,256]{4,3,2,1,0:T(8,128)(2,1)} async-done(((bf16[1,2,6,512,256]{4,3,2,1,0:T(8,128)(2,1)}), bf16[4,2,6,512,256]{4,3,2,1,0:T(8,128)(2,1)}) %all-gather.8.cloned.1.call-update) | async-done | bytes 12582928 | tf_op jit(solution)/shard_map/all_gather | solution.py:86
  361.8 10.6 %fusion.11 = f32[6,512,512,1]{2,1,0,3:T(8,128)} fusion(bf16[4,2,6,512,256]{4,3,2,1,0:T(8,128)(2,1)} %all-gather.8.cloned.1.call-done, bf16[4,2,6,512,256]{4,3,1,2,0:T(8,128)(2,1)} %bitcast.92), kind=kOutput, calls=%fused_computation.21 | convolution fusion | flops 3221225472 | bytes 18874368 | tf_op jit(solution)/shard_map/bmif,bmjf->mij/dot_general | solution.py:76
  372.4 15.0 %fusion.16 = f32[6,1,512,512]{3,2,0,1:T(8,128)} fusion(bf16[4,2,6,512,256]{4,3,1,2,0:T(8,128)(2,1)} %bitcast.93, bf16[4,2,6,512,256]{4,3,2,1,0:T(8,128)(2,1)} %all-gather.8.cloned.1.call-done), kind=kOutput, calls=%fused_computation.29 | convolution fusion | flops 6442450944 | bytes 31457280 | tf_op jit(solution)/shard_map/bpmif,bpmjf->mij/dot_general | solution.py:70
  387.4 0.0 copy-start
  387.4 12.6 %fusion.13 = f32[6,1,512,512]{3,2,0,1:T(8,128)} fusion(f32[6,512,512,1]{2,1,0,3:T(8,128)} %fusion.11, bf16[4,2,6,512,256]{4,3,2,1,0:T(8,128)(2,1)} %all-gather.8.cloned.1.call-done, bf16[4,2,6,512,256]{4,3,1,2,0:T(8,128)(2,1)} %bitcast.94), kind=kOutput, calls=%fused_computation.27 | convolution fusion | flops 3222798336 | bytes 25165824 | tf_op jit(solution)/shard_map/bmif,bmjf->mij/dot_general | solution.py:73
  400.0 0.0 copy-done
  400.0 8.9 %maximum_multiply_fusion = f32[6,2,512,512]{3,2,0,1:T(8,128)} fusion(f32[6,1,512,512]{3,2,0,1:T(8,128)} %fusion.13, f32[6,1,512,512]{3,2,0,1:T(8,128)S(1)} %copy-done), kind=kLoop, calls=%fused_computation | loop fusion | flops 6291456 | bytes 25165824 | tf_op jit(solution)/shard_map/mul | solution.py:80
  408.9 10.9 %copy.44 = f32[6,2,512,512]{3,2,1,0:T(8,128)} copy(f32[6,2,512,512]{3,2,0,1:T(8,128)} %maximum_multiply_fusion) | data formatting | bytes 25165824 | tf_op jit(solution)/shard_map/mul | solution.py:80
Async XLA Ops:
  6.5 182.3 %all-gather.4.cloned.1.call-start = ((), (), s32[]{:S(2)}) async-start(), calls=%async_computation.2 | async-start | bytes 9437184 | tf_op jit(solution)/shard_map/all_gather | solution.py:22
  109.1 137.3 %all-gather.6.cloned.1.call-start = ((), (), s32[]{:S(2)}) async-start(), calls=%async_computation.3 | async-start | bytes 18874368 | tf_op jit(solution)/shard_map/all_gather | solution.py:22
  188.9 172.9 %all-gather.8.cloned.1.call-start = ((), (), s32[]{:S(2)}) async-start(), calls=%async_computation.4 | async-start | bytes 15728640 | tf_op jit(solution)/shard_map/all_gather | solution.py:86
  387.4 12.6 %copy-start = (f32[6,1,512,512]{3,2,0,1:T(8,128)S(1)}, f32[6,1,512,512]{3,2,0,1:T(8,128)}, u32[]{:S(2)}) copy-start(f32[6,1,512,512]{3,2,0,1:T(8,128)} %fusion.16) | copy-start | bytes 18874372
Sparse Core Ops, SparseCore 0:
  109.2 79.5 all-gather.3
  190.5 28.9 all-gather.5
  246.6 115.1 all-gather.7
where the time goes:
time: 427 us; the launch traced here: 426 us
  waiting for transfers between devices  184 us (43%)
  blocking collectives  103 us (24%)
  local copies, waits for them, and re-layouts  49.1 us (11%)
  matrix products  47.5 us (11%)
  other arithmetic  29.4 us (7%)
  between operations  13.2 us (3%)
    all_gather x1, waiting for transfers between devices, correlate(): col_full = lax.all_gather(col_part, 'row', axis=0, tiled=True)  105 us
    all_to_all x2, blocking collectives, exchange_both(): tiles = lax.all_to_all(tiles, axis, split_axis=0, concat_axis=0, tiled=True)  103 us
    all_gather x2, waiting for transfers between devices, gather_in_order(): tiles = lax.all_gather(tiles, axes[k], axis=0, tiled=True)  79.7 us
    add x1, other arithmetic, filter_bank(): filtered + window[tap_index][:, None] * samples[..., tap_index:tap_index...  16.8 us
    dot_general x1, matrix products, products(): jnp.einsum('bpmif,bpmjf->mij', row_full, col_full, preferred_element_type...  15 us
    dot_general x1, matrix products, products(): jnp.einsum('bmif,bmjf->mij', row_full[:, 1], col_full[:, 0], preferred_el...  12.6 us
    mul x1, local copies, waits for them, and re-layouts, products(): return jnp.stack([real_part, imag_part], axis=1) * inverse  10.9 us
    transpose x1, local copies, waits for them, and re-layouts, gather_in_order(): tiles.transpose(*turned, *range(len(turns), tiles.ndim))  10.8 us
  transfers between devices with their start and end apart: 3, of which 2 were waited for; matrix products, arithmetic and copies ran while one was open for 4% of the time, Pallas kernels for 0%

commit v1 on v0

--- a/solution.py
+++ b/solution.py
@@ -83,7 +83,8 @@
 def correlate(pieces):
     row_part, col_part = pieces
     row_full = whole_of(row_part, COL, (0, 1), 0)
-    col_full = lax.all_gather(col_part, "row", axis=0, tiled=True)
+    copies = jnp.concatenate([col_part] * lax.axis_size("row"), axis=0)
+    col_full = lax.all_to_all(copies, "row", 0, 0, tiled=True)
     return products(row_full, col_full)
 
 

time: 427 us -> 462 us (1.082)
  waiting for transfers between devices: 184 us -> 207 us
  starting transfers between devices: 0.08 us -> 6.56 us
    all_to_all x0 -> x1, waiting for transfers between devices: none -> 127 us  [correlate(): col_full = lax.all_to_all(copies, 'row', 0, 0, tiled=True)]
    all_gather x1 -> x0, waiting for transfers between devices: 105 us -> none  [correlate(): col_full = lax.all_gather(col_part, 'row', axis=0, tiled=True)]
    all_to_all x0 -> x1, starting transfers between devices: none -> 6.52 us  [correlate(): col_full = lax.all_to_all(copies, 'row', 0, 0, tiled=True)]
    concatenate x0 -> x1, local copies, waits for them, and re-layouts: none -> 6.27 us  [correlate(): copies = jnp.concatenate([col_part] * lax.axis_size('row'), axis=0)]
  transfers between devices with their start and end apart: 3 -> 3, of which waited for: 2 -> 2; matrix products, arithmetic and copies ran while one was open for 4% -> 5% of each run, Pallas kernels for 0% -> 0%
where the time goes in v1:
time: 462 us; the launch traced here: 460 us
  waiting for transfers between devices  207 us (45%)
  blocking collectives  103 us (22%)
  local copies, waits for them, and re-layouts  53.4 us (12%)
  matrix products  47.9 us (10%)
  other arithmetic  29.4 us (6%)
  between operations  13.5 us (3%)
  starting transfers between devices  6.56 us (1%)
    all_to_all x1, waiting for transfers between devices, correlate(): col_full = lax.all_to_all(copies, 'row', 0, 0, tiled=True)  127 us
    all_to_all x2, blocking collectives, exchange_both(): tiles = lax.all_to_all(tiles, axis, split_axis=0, concat_axis=0, tiled=True)  103 us
    all_gather x2, waiting for transfers between devices, gather_in_order(): tiles = lax.all_gather(tiles, axes[k], axis=0, tiled=True)  79.7 us
    add x1, other arithmetic, filter_bank(): filtered + window[tap_index][:, None] * samples[..., tap_index:tap_index...  16.8 us
    dot_general x1, matrix products, products(): jnp.einsum('bpmif,bpmjf->mij', row_full, col_full, preferred_element_type...  15 us
    dot_general x1, matrix products, products(): jnp.einsum('bmif,bmjf->mij', row_full[:, 1], col_full[:, 0], preferred_el...  12.7 us
    dot_general x1, matrix products, products(): jnp.einsum('bmif,bmjf->mij', row_full[:, 0], col_full[:, 1], preferred_el...  10.9 us
    mul x1, local copies, waits for them, and re-layouts, products(): return jnp.stack([real_part, imag_part], axis=1) * inverse  10.9 us
  transfers between devices with their start and end apart: 3, of which 2 were waited for; matrix products, arithmetic and copies ran while one was open for 5% of the time, Pallas kernels for 0%

profile of v1, /device:TPU:1, one launch (start us, length us, event | category | flops | bytes accessed | tf_op | source)
XLA Modules:
  0.0 460.5 jit_solution(16868476523145801715)
XLA Ops:
  6.5 0.0 all-gather.3.cloned.1.call-start
  6.5 1.0 slice_bitcast_fusion.19
  7.5 3.5 convert_element_type.36
  11.0 16.8 %fusion = f32[2,4,4,64,1024]{4,3,2,1,0:T(8,128)} fusion(f32[2,4,4,64,1031]{4,3,2,1,0:T(8,128)S(1)} %convert_element_type.36, f32[64]{0:T(128)S(1)} %get-tuple-element.14, f32[64]{0:T(128)S(1)} %get-tuple-element.15, f32[64]{0:T(128)S(1)} %get-tuple-element.9, f32[64]{0:T(128)S(1)} %get-tuple-element.10, f32[64]{0:T(128)S(1)} %get-tuple-element.11, ...), kind=kLoop, calls=%fused_computation.2 | loop fusion | flops 31457280 | bytes 75499520 | tf_op jit(solution)/shard_map/add | solution.py:64
  27.8 0.0 copy-start
  27.8 10.6 %reshape.153 = f32[2,4,4,64,4,256]{5,4,3,2,1,0:T(4,128)} reshape(f32[2,4,4,64,1024]{4,3,2,1,0:T(8,128)} %fusion) | data formatting | bytes 16777216 | tf_op jit(solution)/shard_map/reshape | solution.py:106
  38.4 0.0 copy-done
  38.4 0.1 mul.173
  38.5 0.1 copy.30
  38.6 0.2 fusion.26
  38.8 9.3 %bitcast_convert_fusion = bf16[2,8,6,4,4,4,256]{6,1,5,4,3,2,0:T(8,128)(2,1)S(1)} fusion(f32[2,4,4,64,4,256,1,1]{5,4,3,2,1,0,7,6:T(4,128)} %bitcast.103, f32[1,1,8,6,64]{4,2,0,3,1:T(8,128)S(1)} %get-tuple-element.7, f32[1,1,8,6,64]{4,2,0,3,1:T(8,128)S(1)} %get-tuple-element.6, f32[1,1,8,6,64]{4,2,0,3,1:T(8,128)S(1)} %get-tuple-element.5), kind=kOutput, calls=%fused_computation.26 | convolution fusion | flops 2417528832 | bytes 11571200 | tf_op jit(solution)/shard_map/qrsnbf,qpckn->crbpksf/dot_general | solution.py:108
  48.1 2.4 copy.32
  50.5 52.5 %all_to_all.15 = bf16[128,1,1,2,6,1,1,4,256]{8,7,4,3,6,5,2,1,0:T(4,128)(2,1)S(1)} all-to-all(bf16[128,1,1,2,6,1,1,4,256]{8,7,4,3,6,5,2,1,0:T(4,128)(2,1)S(1)} %bitcast.102), channel_id=1, replica_groups=mesh['chan'=8,'row'=4,'col_0'=2,'col_1'=2] {'chan','row','col_0','col_1'}, dimensions={0} | all-to-all | bytes 6291456 | tf_op jit(solution)/shard_map/all_to_all | solution.py:45
  103.0 3.3 copy.34
  106.3 2.2 copy.35
  108.5 0.0 all-gather.3.cloned.1.call-update
  108.5 0.0 all-gather.5.cloned.1.call-start
  108.5 79.7 %all-gather.3.cloned.1.call-done = bf16[2,1,2,6,512,256]{5,4,3,2,1,0:T(8,128)(2,1)} async-done(((bf16[1,1,2,6,512,256]{5,4,3,2,1,0:T(8,128)(2,1)}), bf16[2,1,2,6,512,256]{5,4,3,2,1,0:T(8,128)(2,1)}) %all-gather.3.cloned.1.call-update) | async-done | bytes 6291472 | tf_op jit(solution)/shard_map/all_gather | solution.py:22
  188.2 0.0 all-gather.5.cloned.1.call-update
  188.3 2.4 copy.37
  190.7 50.3 %all_to_all.16 = bf16[128,1,1,2,6,1,1,4,256]{8,7,4,3,6,5,2,1,0:T(4,128)(2,1)S(1)} all-to-all(bf16[128,1,1,2,6,1,1,4,256]{8,7,4,3,6,5,2,1,0:T(4,128)(2,1)S(1)} %bitcast.99), channel_id=1, replica_groups=mesh['chan'=8,'row'=4,'col_0'=2,'col_1'=2] {'chan','row','col_0','col_1'}, dimensions={0} | all-to-all | bytes 6291456 | tf_op jit(solution)/shard_map/all_to_all | solution.py:45
  241.0 3.3 copy.39
  244.2 0.5 copy.40
  244.8 6.3 %concatenate.6 = bf16[4,2,6,512,256]{4,3,1,2,0:T(8,128)(2,1)} broadcast(bf16[2,6,512,256]{3,2,0,1:T(8,128)(2,1)S(1)} %copy.40), dimensions={1,2,3,4} | broadcast | bytes 15728640 | tf_op jit(solution)/shard_map/concatenate | solution.py:86
  251.0 6.5 %all-to-all-start.2 = ((bf16[4,2,6,512,256]{4,3,1,2,0:T(8,128)(2,1)}), bf16[4,2,6,512,256]{4,3,1,2,0:T(8,128)(2,1)}, u32[]{:S(2)}, u32[]{:S(2)}) async-start(bf16[4,2,6,512,256]{4,3,1,2,0:T(8,128)(2,1)} %concatenate.6), calls=%async_computation.2 | async-start | bytes 25165824 | tf_op jit(solution)/shard_map/all_to_all | solution.py:87
  257.5 0.0 all-gather.5.cloned.1.call-done
  257.6 10.5 %copy.36 = bf16[2,2,1,2,6,512,256]{6,5,3,4,1,0,2:T(8,128)(2,1)} copy(bf16[2,2,1,2,6,512,256]{6,5,4,3,0,1,2:T(8,128)(2,1)} %bitcast.91) | data formatting | bytes 25165824 | tf_op jit(solution)/shard_map/transpose | solution.py:26
  268.1 127.2 %all-to-all-done.2 = bf16[4,2,6,512,256]{4,3,1,2,0:T(8,128)(2,1)} async-done(((bf16[4,2,6,512,256]{4,3,1,2,0:T(8,128)(2,1)}), bf16[4,2,6,512,256]{4,3,1,2,0:T(8,128)(2,1)}, u32[]{:S(2)}, u32[]{:S(2)}) %all-to-all-start.2) | async-done | bytes 12582944 | tf_op jit(solution)/shard_map/all_to_all | solution.py:87
  395.2 15.0 %convolution_bitcast_fusion = f32[6,1,512,512]{3,2,0,1:T(8,128)} fusion(bf16[4,2,6,512,256]{4,3,1,2,0:T(8,128)(2,1)} %bitcast.92, bf16[4,2,6,512,256]{4,3,1,2,0:T(8,128)(2,1)} %all-to-all-done.2), kind=kOutput, calls=%fused_computation.27 | convolution fusion | flops 6442450944 | bytes 31457280 | tf_op jit(solution)/shard_map/bpmif,bpmjf->mij/dot_general | solution.py:70
  410.2 0.0 slice-start
  410.2 10.9 %fusion.9 = f32[6,512,512,1]{2,1,0,3:T(8,128)} fusion(bf16[4,2,6,512,256]{4,3,1,2,0:T(8,128)(2,1)} %all-to-all-done.2, bf16[4,2,6,512,256]{4,3,1,2,0:T(8,128)(2,1)} %bitcast.93), kind=kOutput, calls=%fused_computation.19 | convolution fusion | flops 3221225472 | bytes 18874368 | tf_op jit(solution)/shard_map/bmif,bmjf->mij/dot_general | solution.py:76
  421.1 0.0 slice-start.1
  421.1 12.7 %fusion.11 = f32[6,1,512,512]{3,2,0,1:T(8,128)} fusion(f32[6,512,512,1]{2,1,0,3:T(8,128)} %fusion.9, bf16[4,2,6,512,256]{4,3,1,2,0:T(8,128)(2,1)} %all-to-all-done.2, bf16[4,2,6,512,256]{4,3,1,2,0:T(8,128)(2,1)} %bitcast.94), kind=kOutput, calls=%fused_computation.25 | convolution fusion | flops 3222798336 | bytes 25165824 | tf_op jit(solution)/shard_map/bmif,bmjf->mij/dot_general | solution.py:73
  433.8 0.0 slice-done
  433.8 0.0 slice-done.1
  433.8 8.9 %maximum_multiply_fusion = f32[6,2,512,512]{3,2,0,1:T(8,128)} fusion(f32[6,1,512,512]{3,2,0,1:T(8,128)} %fusion.11, f32[6,1,512,512]{3,2,0,1:T(8,128)S(1)} %bitcast.105), kind=kLoop, calls=%fused_computation | loop fusion | flops 6291456 | bytes 25165824 | tf_op jit(solution)/shard_map/mul | solution.py:80
  442.7 10.9 %copy.43 = f32[6,2,512,512]{3,2,1,0:T(8,128)} copy(f32[6,2,512,512]{3,2,0,1:T(8,128)} %maximum_multiply_fusion) | data formatting | bytes 25165824 | tf_op jit(solution)/shard_map/mul | solution.py:80
  (1 shorter events, 0.0 us)
Async XLA Ops:
  6.5 181.7 %all-gather.3.cloned.1.call-start = ((), (), s32[]{:S(2)}) async-start(), calls=%async_computation.3 | async-start | bytes 9437184 | tf_op jit(solution)/shard_map/all_gather | solution.py:22
  27.8 10.6 %copy-start = (s32[48]{0:T(128)S(1)}, s32[48]{0:T(128)}, u32[]{:S(2)}) copy-start(s32[48]{0:T(128)} %param.5) | copy-start | bytes 580
  108.5 149.1 %all-gather.5.cloned.1.call-start = ((), (), s32[]{:S(2)}) async-start(), calls=%async_computation.4 | async-start | bytes 18874368 | tf_op jit(solution)/shard_map/all_gather | solution.py:22
  251.0 144.2 %all-to-all-start.2 = ((bf16[4,2,6,512,256]{4,3,1,2,0:T(8,128)(2,1)}), bf16[4,2,6,512,256]{4,3,1,2,0:T(8,128)(2,1)}, u32[]{:S(2)}, u32[]{:S(2)}) async-start(bf16[4,2,6,512,256]{4,3,1,2,0:T(8,128)(2,1)} %concatenate.6), calls=%async_computation.2 | async-start | bytes 25165824 | tf_op jit(solution)/shard_map/all_to_all | solution.py:87
  410.2 23.6 %slice-start = ((s8[6291456]{0:T(1024)(128)(4,1)}), s8[4194304]{0:T(1024)(128)(4,1)S(1)}, s32[]{:S(2)}) async-start(s8[6291456]{0:T(1024)(128)(4,1)} %bitcast.104), calls=%async_computation.5 | async-start | bytes 8388608
  421.1 12.7 %slice-start.1 = ((s8[6291456]{0:T(1024)(128)(4,1)}), s8[2097152]{0:T(1024)(128)(4,1)S(1)}, s32[]{:S(2)}) async-start(s8[6291456]{0:T(1024)(128)(4,1)} %bitcast.104), calls=%async_computation.6 | async-start | bytes 4194304
Sparse Core Ops, SparseCore 0:
  108.6 79.5 all-gather.2
  189.9 28.9 all-gather.4
